TPU v7x, 32 devices: a whole 2x2x4 slice. The times are simulated.
32 devices in a mesh: grp: 8 (over y, x, core), cli: 4 (over z).
Axes of the slice: x: 2, y: 2, z: 4, core: 2. Of those that a mesh axis runs over, the one named last changes fastest.
Arguments:
- token_ids: int32 [32, 128], P(('grp', 'cli')), may hold values from 0 to 51199
- target_ids: int32 [32, 128], P(('grp', 'cli')), may hold values from 0 to 51199
- segment_ids: int32 [32, 128], P(('grp', 'cli')), may hold values from 0 to 3, never falling along the last dimension, each value on 1 to 64 neighbouring positions
- chosen: int32 [32], P(('grp', 'cli')), may hold values from 0 to 3, as said below
- table: float32 [4, 51200, 768], P(None, ('grp', 'cli')), may hold values from -0.4375 to 0.4375
- table_momentum: float32 [4, 51200, 768], P(None, ('grp', 'cli')), may hold values from -0.00390625 to 0.00390625
- stack: float32 [4, 9344, 768], P(None, ('grp', 'cli')), may hold values from -0.21875 to 0.21875
- stack_momentum: float32 [4, 9344, 768], P(None, ('grp', 'cli')), may hold values from -0.009765625 to 0.009765625
- vectors: float32 [4, 14, 768], replicated, may hold values from -1 to 1.4
- vector_momentum: float32 [4, 14, 768], replicated, may hold values from -0.0546875 to 0.0546875
Outputs:
- loss: float32 [], replicated
- client_losses: float32 [32, 4], P(('grp', 'cli'))
- table_grad: float32 [4, 51200, 768], P(None, ('grp', 'cli'))
- table_momentum_new: float32 [4, 51200, 768], P(None, ('grp', 'cli'))
- table_new: float32 [4, 51200, 768], P(None, ('grp', 'cli'))
- stack_grad: float32 [4, 9344, 768], P(None, ('grp', 'cli'))
- stack_momentum_new: float32 [4, 9344, 768], P(None, ('grp', 'cli'))
- stack_new: float32 [4, 9344, 768], P(None, ('grp', 'cli'))
- vector_grad: float32 [4, 14, 768], replicated
- vector_momentum_new: float32 [4, 14, 768], replicated
- vector_new: float32 [4, 14, 768], replicated
Inputs may be any that keep to these rules, and one draw needn't show every extreme that they name: Every one of the 4 models is chosen by at least one client.
All inputs are finite; a program needn't handle non-finite values.
Results may differ from a plain program's by a relative error of at most 0.0095.
Values may be sent and summed in bfloat16 or wider, within the bound.
A program may use at most 1 GiB of HBM per device.

v0:
```python
import jax
import jax.numpy as jnp
from jax import lax
from jax.sharding import PartitionSpec as P

HEADS = 12
HEAD_DIM = 64
epsilon = 1e-05
momentum_decay = 0.9
table_rate = 4.0
stack_rate = 4.0
vector_rate = 50.0


def layer_norm(inputs, gain_row, shift_row):
    centred = inputs - jnp.mean(inputs, -1, keepdims=True)
    spread = jnp.mean(centred * centred, -1, keepdims=True)
    return centred * lax.rsqrt(spread + epsilon) * gain_row + shift_row


def project(inputs, matrix):
    return lax.dot_general(
        inputs, matrix, (((1,), (1,)), ((), ())), preferred_element_type=jnp.float32
    )


def product(inputs, matrix):
    return jnp.dot(inputs, matrix, preferred_element_type=jnp.float32)


def outer_rows(left, right):
    return lax.dot_general(
        left, right, (((0,), (0,)), ((), ())), preferred_element_type=jnp.float32
    )


def attend(queries, key_rows, segment_row):
    row_count = queries.shape[0]
    head_shape = (row_count, HEADS, HEAD_DIM)
    scores = jnp.einsum(
        "qhd,khd->hqk",
        queries.reshape(head_shape),
        key_rows.reshape(head_shape),
        preferred_element_type=jnp.float32,
    ) * HEAD_DIM ** (-0.5)
    positions = jnp.arange(row_count)
    allowed = (positions[None, :] <= positions[:, None]) & (
        segment_row[None, :] == segment_row[:, None]
    )
    return jax.nn.softmax(jnp.where(allowed[None], scores, -1e30), axis=-1)


def layer_forward(weights, vector_one, inputs, segment_row):
    model_width = inputs.shape[1]
    row_count = inputs.shape[0]
    normed = layer_norm(inputs, vector_one[0], vector_one[1]).astype(jnp.bfloat16)
    queries = (project(normed, weights[0:model_width]) + vector_one[6]).astype(jnp.bfloat16)
    key_rows = project(normed, weights[model_width : 2 * model_width]).astype(jnp.bfloat16)
    values = (project(normed, weights[2 * model_width : 3 * model_width]) + vector_one[7]).astype(
        jnp.bfloat16
    )
    attention = attend(queries, key_rows, segment_row)
    head_shape = (row_count, HEADS, HEAD_DIM)
    mixture = jnp.einsum(
        "hqk,khd->qhd",
        attention.astype(jnp.bfloat16),
        values.reshape(head_shape),
        preferred_element_type=jnp.float32,
    )
    mixture = mixture.reshape(row_count, model_width).astype(jnp.bfloat16)
    middle = inputs + (project(mixture, weights[3 * model_width : 4 * model_width]) + vector_one[8])
    normed_two = layer_norm(middle, vector_one[2], vector_one[3]).astype(jnp.bfloat16)
    hidden = project(normed_two, weights[4 * model_width : 8 * model_width]) + vector_one[
        10:14
    ].reshape(-1)
    active = jax.nn.gelu(hidden, approximate=True).astype(jnp.bfloat16)
    residual = middle + (
        product(active, weights[8 * model_width : 12 * model_width]) + vector_one[9]
    )
    normed_out = layer_norm(residual, vector_one[4], vector_one[5]).astype(jnp.bfloat16)
    return (
        normed,
        queries,
        key_rows,
        values,
        attention,
        mixture,
        middle,
        normed_two,
        hidden,
        active,
        residual,
        normed_out,
    )


def norm_grad(operand, gain_row, shift_row, cotangent):
    outcome, pullback = jax.vjp(layer_norm, operand, gain_row, shift_row)
    return pullback(cotangent)


def gelu_tanh(hidden):
    return jax.nn.gelu(hidden, approximate=True)


def layer_backward(weights, vector_one, inputs, segment_row, grad_out):
    model_width = inputs.shape[1]
    row_count = inputs.shape[0]
    head_shape = (row_count, HEADS, HEAD_DIM)
    scaling = HEAD_DIM ** (-0.5)
    (
        normed,
        queries,
        key_rows,
        values,
        attention,
        mixture,
        middle,
        normed_two,
        hidden,
        active,
        residual,
        normed_out,
    ) = layer_forward(weights, vector_one, inputs, segment_row)
    d_residual, d_gain_out, d_shift_out = norm_grad(
        residual, vector_one[4], vector_one[5], grad_out
    )
    d_outer = d_residual.astype(jnp.bfloat16)
    d_bias_out = jnp.sum(d_outer.astype(jnp.float32), 0)
    grad_down = outer_rows(active, d_outer)
    d_active = project(d_outer, weights[8 * model_width : 12 * model_width])
    gelu_value, gelu_pull = jax.vjp(gelu_tanh, hidden)
    d_hidden = gelu_pull(d_active)[0].astype(jnp.bfloat16)
    d_bias_hidden = jnp.sum(d_hidden.astype(jnp.float32), 0)
    grad_up = outer_rows(d_hidden, normed_two)
    d_normed_two = product(d_hidden, weights[4 * model_width : 8 * model_width])
    d_middle_norm, d_gain_two, d_shift_two = norm_grad(
        middle, vector_one[2], vector_one[3], d_normed_two
    )
    d_middle = d_residual + d_middle_norm
    d_branch = d_middle.astype(jnp.bfloat16)
    d_bias_branch = jnp.sum(d_branch.astype(jnp.float32), 0)
    grad_mix = outer_rows(d_branch, mixture)
    d_mixture = (
        product(d_branch, weights[3 * model_width : 4 * model_width])
        .astype(jnp.bfloat16)
        .reshape(head_shape)
    )
    d_attention = jnp.einsum(
        "qhd,khd->hqk", d_mixture, values.reshape(head_shape), preferred_element_type=jnp.float32
    )
    d_values = jnp.einsum(
        "hqk,qhd->khd",
        attention.astype(jnp.bfloat16),
        d_mixture,
        preferred_element_type=jnp.float32,
    )
    d_values = d_values.reshape(row_count, model_width).astype(jnp.bfloat16)
    d_scores = (
        attention * (d_attention - jnp.sum(attention * d_attention, -1, keepdims=True))
    ).astype(jnp.bfloat16)
    d_queries = (
        jnp.einsum(
            "hqk,khd->qhd",
            d_scores,
            key_rows.reshape(head_shape),
            preferred_element_type=jnp.float32,
        )
        * scaling
    )
    d_queries = d_queries.reshape(row_count, model_width).astype(jnp.bfloat16)
    d_keys = (
        jnp.einsum(
            "hqk,qhd->khd",
            d_scores,
            queries.reshape(head_shape),
            preferred_element_type=jnp.float32,
        )
        * scaling
    )
    d_keys = d_keys.reshape(row_count, model_width).astype(jnp.bfloat16)
    d_joined = jnp.concatenate([d_queries, d_keys, d_values], axis=1)
    grad_joined = outer_rows(d_joined, normed)
    d_normed = product(d_joined, weights[0 : 3 * model_width])
    d_inputs_norm, d_gain_one, d_shift_one = norm_grad(
        inputs, vector_one[0], vector_one[1], d_normed
    )
    d_inputs = d_middle + d_inputs_norm
    stack_rows = jnp.concatenate([grad_joined, grad_mix, grad_up, grad_down, d_inputs], axis=0)
    bias_query = jnp.sum(d_queries.astype(jnp.float32), 0)
    bias_value = jnp.sum(d_values.astype(jnp.float32), 0)
    vector_rows = jnp.concatenate(
        [
            jnp.stack(
                [
                    d_gain_one,
                    d_shift_one,
                    d_gain_two,
                    d_shift_two,
                    d_gain_out,
                    d_shift_out,
                    bias_query,
                    bias_value,
                    d_bias_branch,
                    d_bias_out,
                ]
            ),
            d_bias_hidden.reshape(4, model_width),
        ],
        axis=0,
    )
    return (stack_rows, vector_rows, d_inputs)


def update(weight, momentum, gradient, step_rate):
    renewed = momentum_decay * momentum + gradient
    return (renewed, weight - step_rate * (gradient + momentum_decay * renewed))


def body(
    token_ids,
    target_ids,
    segment_ids,
    chosen,
    table,
    table_momentum,
    stack,
    stack_momentum,
    vectors,
    vector_momentum,
):
    models = table.shape[0]
    block_rows = table.shape[1]
    model_width = table.shape[2]
    seq_len = token_ids.shape[1]
    devices = lax.axis_size(("grp", "cli"))
    group_size = lax.axis_size("cli")
    device_index = lax.axis_index(("grp", "cli"))
    member_index = lax.axis_index("cli")
    token_row = token_ids[0]
    target_row = target_ids[0]
    segment_row = segment_ids[0]
    model_index = chosen[0]
    model_range = jnp.arange(models, dtype=jnp.int32)
    valid_row = jnp.concatenate(
        [(segment_row[:-1] == segment_row[1:]).astype(jnp.float32), jnp.zeros((1,), jnp.float32)]
    )
    count_own = jnp.sum(valid_row)
    own_choice = (model_range == model_index).astype(jnp.float32)
    client_rows = jnp.where(
        (jnp.arange(devices) == device_index)[:, None], (own_choice * count_own)[None, :], 0.0
    )
    client_rows = lax.psum(client_rows, ("grp", "cli"))
    totals = jnp.sum(client_rows, axis=0)
    model_column = jnp.full((seq_len,), model_index, jnp.int32)
    group_tokens, group_targets, group_valid, group_models = (
        lax.all_gather(token_row, "cli", axis=0, tiled=True),
        lax.all_gather(target_row, "cli", axis=0, tiled=True),
        lax.all_gather(valid_row.astype(jnp.int32), "cli", axis=0, tiled=True),
        lax.all_gather(model_column, "cli", axis=0, tiled=True),
    )
    stack_all = lax.all_gather(stack.astype(jnp.bfloat16), ("grp", "cli"), axis=1, tiled=True)
    table_part = lax.all_gather(table.astype(jnp.bfloat16), "grp", axis=1, tiled=True)
    part_rows = table_part.shape[1]

    def locate(global_ids):
        block_index = global_ids // block_rows
        is_owned = block_index % group_size == member_index
        local_rows = jnp.where(
            is_owned, block_index // group_size * block_rows + global_ids % block_rows, 0
        )
        return (is_owned, local_rows)

    token_owned, token_local = locate(group_tokens)
    target_owned, target_local = locate(group_targets)
    picked = jnp.take(table_part, token_local, axis=1)
    embed_terms = jnp.where(token_owned[None, :, None], picked, jnp.zeros_like(picked)).astype(
        jnp.float32
    )
    embedded = lax.psum_scatter(
        embed_terms.astype(jnp.bfloat16), "cli", scatter_dimension=1, tiled=True
    ).astype(jnp.float32)
    inputs = embedded + stack_all[:, 12 * model_width :, :].astype(jnp.float32)

    def forward_one(element):
        return layer_forward(element[0], element[1], element[2], segment_row)[11]

    normed_outs = lax.map(forward_one, (stack_all, vectors, inputs))
    group_outs = lax.all_gather(normed_outs, "cli", axis=1, tiled=True)

    def head_stats(element):
        outs_one, table_one = element
        logits = project(outs_one, table_one)
        highest = jnp.max(logits, -1)
        exp_total = jnp.sum(jnp.exp(logits - highest[:, None]), -1)
        target_logit = jnp.where(
            target_owned, jnp.take_along_axis(logits, target_local[:, None], axis=1)[:, 0], 0.0
        )
        return (highest, exp_total, target_logit)

    highests, exp_totals, target_logits = lax.map(head_stats, (group_outs, table_part))
    highest_all = lax.pmax(highests, "cli")
    sum_all, target_all = (
        lax.psum((exp_totals * jnp.exp(highests - highest_all)).astype(jnp.bfloat16), "cli").astype(
            jnp.float32
        ),
        lax.psum(target_logits.astype(jnp.bfloat16), "cli").astype(jnp.float32),
    )
    log_totals = highest_all + jnp.log(sum_all)
    token_loss = log_totals - target_all
    own_loss = lax.dynamic_slice_in_dim(token_loss, member_index * seq_len, seq_len, 1)
    client_losses = (jnp.sum(own_loss * valid_row[None, :], axis=1) / count_own)[None, :]
    own_total = jnp.sum(own_choice * totals)
    loss_term = jnp.sum(jnp.sum(own_loss * own_choice[:, None], 0) * valid_row) / own_total
    group_totals = jnp.sum(
        jnp.where(group_models[:, None] == model_range[None, :], totals[None, :], 0.0), axis=1
    )
    token_weight = group_valid.astype(jnp.float32) / group_totals
    vocab_range = jnp.arange(part_rows)

    def head_back(grad_table, block_index):
        block_start = block_index * seq_len
        model_pick = group_models[block_start]
        outs_block = lax.dynamic_slice(
            group_outs, (model_pick, block_start, 0), (1, seq_len, model_width)
        )[0]
        table_one = lax.dynamic_index_in_dim(table_part, model_pick, 0, keepdims=False)
        logits = project(outs_block, table_one)
        lse_block = lax.dynamic_slice(log_totals, (model_pick, block_start), (1, seq_len))[0]
        softmax_rows = jnp.exp(logits - lse_block[:, None])
        target_block = lax.dynamic_slice_in_dim(target_local, block_start, seq_len)
        owned_block = lax.dynamic_slice_in_dim(target_owned, block_start, seq_len)
        weight_block = lax.dynamic_slice_in_dim(token_weight, block_start, seq_len)
        target_hit = (
            (vocab_range[None, :] == target_block[:, None]) & owned_block[:, None]
        ).astype(jnp.float32)
        d_logits = (weight_block[:, None] * (softmax_rows - target_hit)).astype(jnp.bfloat16)
        d_outs = product(d_logits, table_one)
        grad_rows = outer_rows(d_logits, outs_block)
        current = lax.dynamic_index_in_dim(grad_table, model_pick, 0, keepdims=False)
        grad_table = lax.dynamic_update_index_in_dim(grad_table, current + grad_rows, model_pick, 0)
        return (grad_table, d_outs)

    head_init = jnp.zeros((models, part_rows, model_width), jnp.float32)
    grad_table, d_outs = lax.scan(head_back, head_init, jnp.arange(group_size))
    d_final = lax.psum_scatter(
        d_outs.reshape(group_size * seq_len, model_width), "cli", scatter_dimension=0, tiled=True
    )
    stack_one = lax.dynamic_index_in_dim(stack_all, model_index, 0, keepdims=False)
    vector_one = lax.dynamic_index_in_dim(vectors, model_index, 0, keepdims=False)
    inputs_one = lax.dynamic_index_in_dim(inputs, model_index, 0, keepdims=False)
    stack_rows, vector_rows, d_inputs = layer_backward(
        stack_one, vector_one, inputs_one, segment_row, d_final
    )
    group_grads = lax.all_gather(d_inputs.astype(jnp.bfloat16), "cli", axis=0, tiled=True)
    drop_rows = jnp.where(token_owned, token_local, part_rows)
    grad_table = grad_table.at[group_models, drop_rows].add(
        group_grads.astype(jnp.float32), mode="drop"
    )
    table_grad = lax.psum_scatter(
        grad_table.astype(jnp.bfloat16), "grp", scatter_dimension=1, tiled=True
    ).astype(jnp.float32)
    masked = jnp.where((model_range == model_index)[:, None, None], stack_rows[None], 0.0)
    stack_grad = lax.psum_scatter(masked, ("grp", "cli"), scatter_dimension=1, tiled=True)
    vector_masked = jnp.where((model_range == model_index)[:, None, None], vector_rows[None], 0.0)
    vector_grad, loss = lax.psum((vector_masked, loss_term), ("grp", "cli"))
    table_momentum_new, table_new = update(table, table_momentum, table_grad, table_rate)
    stack_momentum_new, stack_new = update(stack, stack_momentum, stack_grad, stack_rate)
    vector_momentum_new, vector_new = update(vectors, vector_momentum, vector_grad, vector_rate)
    return (
        loss,
        client_losses,
        table_grad,
        table_momentum_new,
        table_new,
        stack_grad,
        stack_momentum_new,
        stack_new,
        vector_grad,
        vector_momentum_new,
        vector_new,
    )


def solution(mesh):
    placed = (
        P(("grp", "cli"), None),
        P(("grp", "cli"), None),
        P(("grp", "cli"), None),
        P(("grp", "cli")),
        P(None, ("grp", "cli"), None),
        P(None, ("grp", "cli"), None),
        P(None, ("grp", "cli"), None),
        P(None, ("grp", "cli"), None),
        P(),
        P(),
    )
    return jax.shard_map(
        body,
        mesh=mesh,
        in_specs=placed,
        out_specs=(
            P(),
            P(("grp", "cli"), None),
            P(None, ("grp", "cli"), None),
            P(None, ("grp", "cli"), None),
            P(None, ("grp", "cli"), None),
            P(None, ("grp", "cli"), None),
            P(None, ("grp", "cli"), None),
            P(None, ("grp", "cli"), None),
            P(),
            P(),
            P(),
        ),
        check_vma=False,
    )
```

profile of v0, /device:TPU:0, one launch (start us, length us, event | category | flops | bytes accessed | tf_op | source)
XLA Modules:
  0.0 3884.0 jit_solution(11815534252745579856)
XLA Ops:
  7.2 29.7 copy.117
  40.9 12.6 all-gather
  54.1 338.0 %all-gather.8.cloned.1.call-done = bf16[4,12800,768]{2,0,1:T(4,128)(2,1)} async-done(((bf16[4,1600,768]{2,0,1:T(4,128)(2,1)}), bf16[4,12800,768]{2,0,1:T(4,128)(2,1)}) %all-gather.8.cloned.1.call-update) | async-done | bytes 78643216 | tf_op jit(solution)/shard_map/all_gather | solution.py:263
  392.1 17.6 gather_fusion.1
  415.7 289.6 %all-gather.10.cloned.1.call-done = bf16[4,9344,768]{2,0,1:T(4,128)(2,1)} async-done(((bf16[4,292,768]{2,0,1:T(4,128)(2,1)}), bf16[4,9344,768]{2,0,1:T(4,128)(2,1)}) %all-gather.10.cloned.1.call-update) | async-done | bytes 57409552 | tf_op jit(solution)/shard_map/all_gather | solution.py:262
  705.3 38.5 copy.97
  743.9 83.7 %all-reduce.9.cloned.1.call-done = bf16[4,512,768]{2,0,1:T(4,128)(2,1)} async-done(((bf16[4,512,768]{2,0,1:T(4,128)(2,1)}), bf16[4,512,768]{2,0,1:T(4,128)(2,1)}) %all-reduce.9.cloned.1.call-update) | async-done | bytes 3145744
  830.3 68.9 %while.37 = (s32[]{:T(128)}, bf16[4,128,768]{2,1,0:T(8,128)(2,1)}, f32[4,128,768]{2,1,0:T(8,128)S(1)}, f32[4,14,768]{2,0,1:T(4,128)S(1)}, bf16[4,9344,768]{2,1,0...) while((s32[]{:T(128)}, bf16[4,128,768]{2,1,0:T(8,128)(2,1)}, ...), condition=%wide.region_10.11_spmd, body=%wide.region_1.10_spmd.sunk | while | flops 1896827008 | bytes 24394716 | solution.py:288
  901.4 42.1 %psum.37 = f32[32,4]{0,1:T(4,128)S(1)} all-reduce(f32[32,4]{0,1:T(4,128)S(1)} %broadcast_select_fusion.2), channel_id=1, replica_groups=mesh['grp'=8,'cli'=4] {'grp','cli'}, use_global_device_ids=true, to_apply=%region_21.22 | all-reduce | flops 128 | bytes 1024 | tf_op jit(solution)/shard_map/psum | solution.py:253
  943.7 11.3 all-gather.1
  967.8 51.4 %copy.99 = bf16[4,12800,768]{2,1,0:T(8,128)(2,1)} copy(bf16[4,12800,768]{2,0,1:T(4,128)(2,1)} %all-gather.8.cloned.1.call-done) | data formatting | bytes 157286400 | tf_op jit(solution)/shard_map/while | solution.py:301
  1020.5 166.1 %while.38 = (s32[]{:T(128)}, f32[4,512]{1,0:T(4,128)S(1)}, f32[4,512]{1,0:T(4,128)S(1)}, bf16[4,512]{1,0:T(4,128)(2,1)S(1)}, bf16[4,512,768]{2,1,0:T(8,128)(2,1)...) while((s32[]{:T(128)}, f32[4,512]{1,0:T(4,128)S(1)}, ...), condition=%wide.region_14.15_spmd, body=%wide.region_11.14_spmd.sunk | while | flops 10086000640 | bytes 72927864 | solution.py:301
  1020.5 21.3 fusion.288
  1041.9 10.8 exponential_reduce_fusion.2
  1062.0 21.3 fusion.288
  1083.4 10.8 exponential_reduce_fusion.2
  1103.6 21.3 fusion.288
  1124.9 10.8 exponential_reduce_fusion.2
  1145.1 21.3 fusion.288
  1166.4 10.8 exponential_reduce_fusion.2
  1186.6 12.7 pmax.7
  1209.8 9.5 all-gather.3
  1219.3 48.1 %broadcast_in_dim.238 = f32[4,12800,768]{2,1,0:T(8,128)} broadcast(f32[]{:T(128)} %constant.231.clone.1), dimensions={} | broadcast | bytes 157286400 | tf_op jit(solution)/shard_map/broadcast_in_dim | solution.py:344
  1267.4 320.8 %while.39 = (s32[]{:T(128)}, f32[4,12800,768]{2,1,0:T(8,128)}, f32[4,128,768]{2,1,0:T(8,128)}, s32[4]{0:T(128)S(1)}, s32[512]{0:T(512)S(1)}, /*index=5*/f32[512]...) while((s32[]{:T(128)}, f32[4,12800,768]{2,1,0:T(8,128)}, ...), condition=%wide.region_28.29_spmd.clone, body=%wide.region_27.28_spmd.clone.sunk | while | flops 7571046400 | bytes 207235280 | solution.py:345
  1271.2 26.9 constant_dynamic-slice_fusion.30
  1299.8 10.5 fusion.296
  1310.3 28.5 bitcast_dynamic-update-slice_fusion.2
  1338.8 8.8 fusion.297
  1351.4 26.9 constant_dynamic-slice_fusion.30
  1379.9 10.5 fusion.296
  1390.4 28.6 bitcast_dynamic-update-slice_fusion.2
  1419.0 8.8 fusion.297
  1431.6 26.9 constant_dynamic-slice_fusion.30
  1460.1 10.5 fusion.296
  1470.6 28.6 bitcast_dynamic-update-slice_fusion.2
  1511.8 26.9 constant_dynamic-slice_fusion.30
  1540.3 10.5 fusion.296
  1550.9 28.6 bitcast_dynamic-update-slice_fusion.2
  1607.4 14.9 reduce-scatter.3.cloned.1.call-done
  1654.4 9.2 copy-done.2
  1665.7 46.9 %broadcast_select_fusion = f32[4,9344,768]{2,0,1:T(4,128)} fusion(f32[9344,768]{1,0:T(8,128)} %get-tuple-element.391, pred[4]{0:T(512)(128)(4,1)S(1)} %copy-done.60), kind=kLoop, calls=%fused_computation.140 | loop fusion | flops 28704768 | bytes 143523840 | tf_op jit(solution)/shard_map/jit(_where)/select_n | solution.py:363
  1713.2 18.4 all_gather.31
  1731.8 75.4 %scatter_fusion = f32[4,12800,768]{2,1,0:T(8,128)} fusion(f32[4,12800,768]{2,1,0:T(8,128)} %get-tuple-element.154, s32[512]{0:T(512)S(1)} %bitcast.358, f32[512,768]{1,0:T(8,128)S(1)} %convert_element_type.245), kind=kCustom, calls=%fused_computation.2 | custom fusion | flops 393216 | bytes 4722688 | tf_op jit(solution)/shard_map/scatter-add | solution.py:357
  1807.2 77.9 %convert_element_type.246 = bf16[4,12800,768]{2,1,0:T(8,128)(2,1)} convert(f32[4,12800,768]{2,1,0:T(8,128)} %scatter_fusion) | non-fusion elementwise | flops 39321600 | bytes 235929600 | tf_op jit(solution)/shard_map/convert_element_type | solution.py:361
  1887.7 39.6 %psum.38 = f32[]{:T(128)} all-reduce(f32[]{:T(128)S(6)} %div.149), channel_id=1, replica_groups=mesh['grp'=8,'cli'=4] {'grp','cli'}, use_global_device_ids=true, to_apply=%region_24.25 | all-reduce | flops 1 | bytes 8 | tf_op jit(solution)/shard_map/psum | solution.py:366
  1930.1 1468.0 %all-reduce.11.cloned.1.call-done = f32[4,9344,768]{2,0,1:T(4,128)} async-done(((f32[4,9344,768]{2,0,1:T(4,128)}), f32[4,9344,768]{2,0,1:T(4,128)}) %all-reduce.11.cloned.1.call-update) | async-done | bytes 114819088
  3406.4 432.9 %reduce-scatter.5.cloned.1.call-done = bf16[4,1600,768]{2,1,0:T(8,128)(2,1)} async-done(((bf16[4,12800,768]{2,1,0:T(8,128)(2,1)}), bf16[4,1600,768]{2,1,0:T(8,128)(2,1)}) %reduce-scatter.5.cloned.1.call-update) | async-done | bytes 9830416 | tf_op jit(solution)/shard_map/reduce_scatter | solution.py:360
  3839.3 37.0 multiply_subtract_fusion
  (447 shorter events, 239.9 us)
Async XLA Ops:
  7.2 384.9 %all-gather.8.cloned.1.call-start = ((), (), s32[]{:S(2)}) async-start(), calls=%async_computation.2 | async-start | bytes 88473600 | tf_op jit(solution)/shard_map/all_gather | solution.py:263
  36.9 668.4 %all-gather.10.cloned.1.call-start = ((), (), s32[]{:S(2)}) async-start(), calls=%async_computation.3 | async-start | bytes 59203584 | tf_op jit(solution)/shard_map/all_gather | solution.py:262
  40.9 786.7 %all-reduce.9.cloned.1.call-start = ((), (), s32[]{:S(2)}) async-start(), calls=%async_computation.8 | async-start | bytes 6291456
  414.2 606.2 %all-gather.12.cloned.1.call-start = ((), (), s32[]{:S(2)}) async-start(), calls=%async_computation.4 | async-start | bytes 3932160 | tf_op jit(solution)/shard_map/all_gather | solution.py:289
  743.8 86.4 %copy-start.6 = (f32[4,14,768]{2,0,1:T(4,128)S(1)}, f32[4,14,768]{2,0,1:T(4,128)}, u32[]{:S(2)}) copy-start(f32[4,14,768]{2,0,1:T(4,128)} %param.24) | copy-start | bytes 516100
  743.9 86.4 %copy-start.19 = (s32[1,128]{1,0:T(1,128)S(1)}, s32[1,128]{1,0:T(1,128)}, u32[]{:S(2)}) copy-start(s32[1,128]{1,0:T(1,128)} %param.18) | copy-start | bytes 1540
  830.3 113.4 %copy-start.66 = (s32[1,128]{1,0:T(1,128)S(1)}, s32[1,128]{1,0:T(1,128)}, u32[]{:S(2)}) copy-start(s32[1,128]{1,0:T(1,128)} %param.17) | copy-start | bytes 1540
  899.2 120.4 %copy-start = (f32[4,128,768]{2,1,0:T(8,128)}, f32[4,128,768]{2,1,0:T(8,128)S(1)}, u32[]{:S(2)}) copy-start(f32[4,128,768]{2,1,0:T(8,128)S(1)} %get-tuple-element.767) | copy-start | bytes 4718596
  899.2 723.1 %reduce-scatter.3.cloned.1.call-start = ((), (), s32[]{:S(2)}) async-start(), calls=%async_computation.5 | async-start | bytes 1966080 | tf_op jit(solution)/shard_map/reduce_scatter | solution.py:346
  943.6 22.2 copy-start.58
  962.7 56.5 %copy-start.25 = (s32[4,1,128]{2,1,0:T(1,128)}, s32[4,1,128]{2,1,0:T(1,128)S(1)}, u32[]{:S(2)}) copy-start(s32[4,1,128]{2,1,0:T(1,128)S(1)} %all-gather.2) | copy-start | bytes 6148
  963.4 56.2 %copy-start.17 = (f32[768]{0:T(1024)}, f32[768]{0:T(1024)S(1)}, u32[]{:S(2)}) copy-start(f32[768]{0:T(1024)S(1)} %get-tuple-element.306) | copy-start | bytes 9220
  963.4 56.2 %copy-start.21 = (f32[768]{0:T(1024)}, f32[768]{0:T(1024)S(1)}, u32[]{:S(2)}) copy-start(f32[768]{0:T(1024)S(1)} %get-tuple-element.305) | copy-start | bytes 9220
  1020.5 188.0 %copy-start.70 = (f32[4]{0:T(128)S(1)}, f32[4]{0:T(128)}, u32[]{:S(2)}) copy-start(f32[4]{0:T(128)} %fusion.185) | copy-start | bytes 52
  1020.5 188.0 %copy-start.71 = (f32[128]{0:T(128)S(1)}, f32[128]{0:T(128)}, u32[]{:S(2)}) copy-start(f32[128]{0:T(128)} %pad_maximum_fusion.3) | copy-start | bytes 1540
  1020.5 188.6 %copy-start.68 = (f32[127]{0:T(128)S(1)}, f32[127]{0:T(128)}, u32[]{:S(2)}) copy-start(f32[127]{0:T(128)} %copy-done.67) | copy-start | bytes 1528
  1020.5 198.8 %copy-start.50 = (f32[512]{0:T(512)S(1)}, f32[512]{0:T(512)}, u32[]{:S(2)}) copy-start(f32[512]{0:T(512)} %select_reduce_fusion) | copy-start | bytes 6148
  1186.6 80.8 %copy-start.27 = (pred[512]{0:T(512)(128)(4,1)}, pred[512]{0:T(512)(128)(4,1)S(1)}, u32[]{:S(2)}) copy-start(pred[512]{0:T(512)(128)(4,1)S(1)} %get-tuple-element.790) | copy-start | bytes 1540
  1219.3 48.1 %copy-start.26 = (s32[4,1,128]{2,1,0:T(1,128)S(1)}, s32[4,1,128]{2,1,0:T(1,128)}, u32[]{:S(2)}) copy-start(s32[4,1,128]{2,1,0:T(1,128)} %copy-done.25) | copy-start | bytes 6148
  1267.4 321.3 %copy-start.5 = (bf16[128,768]{1,0:T(8,128)(2,1)S(1)}, bf16[128,768]{1,0:T(8,128)(2,1)}, u32[]{:S(2)}) copy-start(bf16[128,768]{1,0:T(8,128)(2,1)} %fusion.131) | copy-start | bytes 589828
  1267.4 321.3 %copy-start.33 = (f32[768]{0:T(1024)S(1)}, f32[768]{0:T(1024)}, u32[]{:S(2)}) copy-start(f32[768]{0:T(1024)} %get-tuple-element.304) | copy-start | bytes 9220
  1271.2 28.5 copy-start.28
  1351.3 28.5 copy-start.28
  1431.6 28.5 copy-start.28
  1511.8 28.5 copy-start.28
  1588.2 6.7 copy-start.38
  1588.2 340.1 %all-reduce.7.cloned.1.call-start = ((), (), s32[]{:S(2)}) async-start(), calls=%async_computation.7 | async-start | bytes 344064 | tf_op jit(solution)/shard_map/psum | solution.py:366
  1590.7 6.1 copy-start.15
  1596.2 6.9 copy-start.47
  1598.8 36.6 copy-start.45
  1603.1 19.2 copy-start.23
  1636.4 7.1 copy-start.48
  1652.5 11.1 copy-start.40
  1652.5 11.2 copy-start.39
  1652.5 11.2 copy-start.35
  1652.5 11.2 copy-start.34
  1652.5 11.3 copy-start.51
  1652.5 11.3 copy-start.37
  1652.5 11.3 copy-start.36
  1652.5 11.3 copy-start.44
  1652.6 11.4 copy-start.60
  1654.1 9.5 copy-start.2
  1664.8 1733.3 %all-reduce.11.cloned.1.call-start = ((), (), s32[]{:S(2)}) async-start(), calls=%async_computation.9 | async-start | bytes 229638144
  1712.6 2126.7 %reduce-scatter.5.cloned.1.call-start = ((), (), s32[]{:S(2)}) async-start(), calls=%async_computation.6 | async-start | bytes 88473600 | tf_op jit(solution)/shard_map/reduce_scatter | solution.py:360
  1885.1 42.1 %copy-start.69 = (f32[4]{0:T(128)S(1)}, f32[4]{0:T(128)}, u32[]{:S(2)}) copy-start(f32[4]{0:T(128)} %get-tuple-element.308) | copy-start | bytes 52
  1885.1 43.2 %copy-start.7 = (f32[4,14,768]{2,0,1:T(4,128)S(1)}, f32[4,14,768]{2,0,1:T(4,128)}, u32[]{:S(2)}) copy-start(f32[4,14,768]{2,0,1:T(4,128)} %param.24) | copy-start | bytes 516100
  1885.1 43.2 %copy-start.16 = (f32[4,14,768]{2,0,1:T(4,128)S(1)}, f32[4,14,768]{2,0,1:T(4,128)}, u32[]{:S(2)}) copy-start(f32[4,14,768]{2,0,1:T(4,128)} %param.25) | copy-start | bytes 516100
  3406.4 469.9 %copy-start.14 = (f32[4,14,768]{2,0,1:T(4,128)S(1)}, f32[4,14,768]{2,0,1:T(4,128)}, u32[]{:S(2)}) copy-start(f32[4,14,768]{2,0,1:T(4,128)} %all-reduce.7.cloned.1.call-done) | copy-start | bytes 516100
  (36 other events, 94.0 us)
Sparse Core Ops, SparseCore 0:
  37.1 355.0 all-gather.7
  395.5 309.8 all-gather.9
  708.3 119.2 all-reduce.8
  899.3 63.4 all-gather.11
  1588.3 33.9 reduce-scatter.2
  1664.9 121.1 all-reduce.6
  1792.5 1605.5 all-reduce.10
  3402.2 437.0 reduce-scatter.4
where the time goes:
time: 3900 us; the launch traced here: 3880 us
  waiting for transfers between devices  2630 us (67%)
  matrix products  378 us (10%)
  local copies, waits for them, and re-layouts  356 us (9%)
  other arithmetic  330 us (8%)
  blocking collectives  162 us (4%)
    unnamed x10, waiting for transfers between devices  1550 us
    reduce_scatter x1, waiting for transfers between devices, body(): lax.psum_scatter(grad_table.astype(jnp.bfloat16), 'grp', scatter_dimensio...  433 us
    all_gather x1, waiting for transfers between devices, body(): lax.all_gather(table.astype(jnp.bfloat16), 'grp', axis=1, tiled=True)  338 us
    all_gather x1, waiting for transfers between devices, body(): lax.all_gather(stack.astype(jnp.bfloat16), ('grp', 'cli'), axis=1, tiled=...  290 us
    dot_general x30, matrix products, project(): lax.dot_general(inputs, matrix, (((1,), (1,)), ((), ())), preferred_eleme...  173 us
    dot_general x8, matrix products, outer_rows(): lax.dot_general(left, right, (((0,), (0,)), ((), ())), preferred_element_...  119 us
    dynamic_slice x4, local copies, waits for them, and re-layouts, head_back(): lax.dynamic_index_in_dim(grad_table, model_pick, 0, keepdims=False)  108 us
  transfers between devices with their start and end apart: 8, of which 6 were waited for; matrix products, arithmetic and copies ran while one was open for 9% of the time, Pallas kernels for 0%

commit v1 on v0

--- a/solution.py
+++ b/solution.py
@@ -260,7 +260,20 @@
         lax.all_gather(model_column, "cli", axis=0, tiled=True),
     )
     stack_all = lax.all_gather(stack.astype(jnp.bfloat16), ("grp", "cli"), axis=1, tiled=True)
-    table_part = lax.all_gather(table.astype(jnp.bfloat16), "grp", axis=1, tiled=True)
+    x = table.astype(jnp.bfloat16)
+    ways, here, step = (lax.axis_size("grp"), lax.axis_index("grp"), x.shape[1])
+    shape = [n * ways if d == 1 else n for d, n in enumerate(x.shape)]
+    full = lax.dynamic_update_slice_in_dim(jnp.zeros(shape, x.dtype), x, here * step, axis=1)
+    going_up = going_down = x
+    for far in range(1, ways // 2 + 1):
+        going_up = lax.ppermute(going_up, "grp", [(d, (d + 1) % ways) for d in range(ways)])
+        full = lax.dynamic_update_slice_in_dim(full, going_up, (here - far) % ways * step, axis=1)
+        if 2 * far < ways:
+            going_down = lax.ppermute(going_down, "grp", [(d, (d - 1) % ways) for d in range(ways)])
+            full = lax.dynamic_update_slice_in_dim(
+                full, going_down, (here + far) % ways * step, axis=1
+            )
+    table_part = full
     part_rows = table_part.shape[1]
 
     def locate(global_ids):

time: 3900 us -> 4060 us (1.041)
  local copies, waits for them, and re-layouts: 356 us -> 449 us
  waiting for transfers between devices: 2630 us -> 2680 us
    ppermute x0 -> x7, waiting for transfers between devices: none -> 665 us  [the longest x4 665 us: body(): lax.ppermute(going_up, 'grp', [(d, (d + 1) % ways) for d in range(ways)])]
    reduce_scatter x1, waiting for transfers between devices: 433 us -> 0.01 us  [body(): lax.psum_scatter(grad_table.astype(jnp.bfloat16), 'grp', scatter_dimensio...]
    all_gather x1 -> x0, waiting for transfers between devices: 338 us -> none  [body(): lax.all_gather(table.astype(jnp.bfloat16), 'grp', axis=1, tiled=True)]
    unnamed x10 -> x9, waiting for transfers between devices: 1550 us -> 1810 us
    all_gather x1, waiting for transfers between devices: 290 us -> 194 us  [body(): lax.all_gather(stack.astype(jnp.bfloat16), ('grp', 'cli'), axis=1, tiled=...]
    dynamic_update_slice x0 -> x8, local copies, waits for them, and re-layouts: none -> 86.9 us  [the longest x4 36.6 us: body(): lax.dynamic_update_slice_in_dim(full, going_up, (here - far) % ways * ste...]
  transfers between devices with their start and end apart: 8 -> 14, of which waited for: 6 -> 8; matrix products, arithmetic and copies ran while one was open for 9% -> 9% of each run, Pallas kernels for 0% -> 0%
where the time goes in v1:
time: 4060 us; the launch traced here: 4040 us
  waiting for transfers between devices  2680 us (66%)
  local copies, waits for them, and re-layouts  449 us (11%)
  matrix products  378 us (9%)
  other arithmetic  330 us (8%)
  blocking collectives  162 us (4%)
    unnamed x9, waiting for transfers between devices  1810 us
    ppermute x4, waiting for transfers between devices, body(): lax.ppermute(going_up, 'grp', [(d, (d + 1) % ways) for d in range(ways)])  665 us
    all_gather x1, waiting for transfers between devices, body(): lax.all_gather(stack.astype(jnp.bfloat16), ('grp', 'cli'), axis=1, tiled=...  194 us
    dot_general x30, matrix products, project(): lax.dot_general(inputs, matrix, (((1,), (1,)), ((), ())), preferred_eleme...  174 us
    dot_general x8, matrix products, outer_rows(): lax.dot_general(left, right, (((0,), (0,)), ((), ())), preferred_element_...  119 us
    dynamic_slice x4, local copies, waits for them, and re-layouts, head_back(): lax.dynamic_index_in_dim(grad_table, model_pick, 0, keepdims=False)  108 us
  transfers between devices with their start and end apart: 14, of which 8 were waited for; matrix products, arithmetic and copies ran while one was open for 9% of the time, Pallas kernels for 0%

profile of v1, /device:TPU:0, one launch (start us, length us, event | category | flops | bytes accessed | tf_op | source)
XLA Modules:
  0.0 4042.8 jit_solution(12684281686443242338)
XLA Ops:
  8.1 30.5 broadcast_in_dim.235
  38.6 26.6 constant_dynamic-update-slice_fusion.7
  68.4 209.2 %collective-permute-done = bf16[4,1600,768]{2,0,1:T(4,128)(2,1)S(1)} collective-permute-done((bf16[4,1600,768]{2,0,1:T(4,128)(2,1)S(1)}, bf16[4,1600,768]{2,0,1:T(4,128)(2,1)S(1)}, u32[]{:S(2)}, u32[]{:S(2)}) %collective-permute-start) | collective-permute-done | bytes 9830432 | tf_op jit(solution)/shard_map/ppermute | solution.py:269
  284.2 209.2 %collective-permute-done.2 = bf16[4,1600,768]{2,0,1:T(4,128)(2,1)S(1)} collective-permute-done((bf16[4,1600,768]{2,0,1:T(4,128)(2,1)S(1)}, bf16[4,1600,768]{2,0,1:T(4,128)(2,1)S(1)}, u32[]{:S(2)}, u32[]{:S(2)}) %collective-permute-start.2) | collective-permute-done | bytes 9830432 | tf_op jit(solution)/shard_map/ppermute | solution.py:269
  498.7 206.0 %collective-permute-done.4 = bf16[4,1600,768]{2,0,1:T(4,128)(2,1)} collective-permute-done((bf16[4,1600,768]{2,0,1:T(4,128)(2,1)S(1)}, bf16[4,1600,768]{2,0,1:T(4,128)(2,1)}, u32[]{:S(2)}, u32[]{:S(2)}) %collective-permute-start.4) | collective-permute-done | bytes 9830432 | tf_op jit(solution)/shard_map/ppermute | solution.py:269
  708.1 14.0 all-gather
  722.8 13.0 constant_dynamic-update-slice_fusion.6
  774.0 40.3 collective-permute-done.6
  823.5 17.6 gather_fusion.1
  851.0 202.9 %all-reduce.9.cloned.1.call-done = bf16[4,512,768]{2,0,1:T(4,128)(2,1)} async-done(((bf16[4,512,768]{2,0,1:T(4,128)(2,1)}), bf16[4,512,768]{2,0,1:T(4,128)(2,1)}) %all-reduce.9.cloned.1.call-update) | async-done | bytes 3145744
  1055.3 193.6 %all-gather.7.cloned.1.call-done = bf16[4,9344,768]{2,0,1:T(4,128)(2,1)} async-done(((bf16[4,292,768]{2,0,1:T(4,128)(2,1)}), bf16[4,9344,768]{2,0,1:T(4,128)(2,1)}) %all-gather.7.cloned.1.call-update) | async-done | bytes 57409552 | tf_op jit(solution)/shard_map/all_gather | solution.py:262
  1248.9 37.9 copy.97
  1288.1 68.9 %while.37 = (s32[]{:T(128)}, bf16[4,128,768]{2,1,0:T(8,128)(2,1)}, f32[4,128,768]{2,1,0:T(8,128)S(1)}, f32[4,14,768]{2,0,1:T(4,128)S(1)}, bf16[4,9344,768]{2,1,0...) while((s32[]{:T(128)}, bf16[4,128,768]{2,1,0:T(8,128)(2,1)}, ...), condition=%wide.region_10.11_spmd, body=%wide.region_1.10_spmd.sunk | while | flops 1896827008 | bytes 24394716 | solution.py:301
  1359.2 41.2 %psum.37 = f32[32,4]{0,1:T(4,128)S(1)} all-reduce(f32[32,4]{0,1:T(4,128)S(1)} %broadcast_select_fusion.2), channel_id=1, replica_groups=mesh['grp'=8,'cli'=4] {'grp','cli'}, use_global_device_ids=true, to_apply=%region_21.22 | all-reduce | flops 128 | bytes 1024 | tf_op jit(solution)/shard_map/psum | solution.py:253
  1400.5 11.3 all-gather.1
  1424.7 51.4 %copy.99 = bf16[4,12800,768]{2,1,0:T(8,128)(2,1)} copy(bf16[4,12800,768]{2,0,1:T(4,128)(2,1)} %constant_dynamic-update-slice_fusion) | data formatting | bytes 157286400 | tf_op jit(solution)/shard_map/while | solution.py:314
  1477.4 166.1 %while.38 = (s32[]{:T(128)}, f32[4,512]{1,0:T(4,128)S(1)}, f32[4,512]{1,0:T(4,128)S(1)}, bf16[4,512]{1,0:T(4,128)(2,1)S(1)}, bf16[4,512,768]{2,1,0:T(8,128)(2,1)...) while((s32[]{:T(128)}, f32[4,512]{1,0:T(4,128)S(1)}, ...), condition=%wide.region_14.15_spmd, body=%wide.region_11.14_spmd.sunk | while | flops 10086000640 | bytes 72927864 | solution.py:314
  1477.4 21.3 fusion.288
  1498.7 10.8 exponential_reduce_fusion.2
  1518.9 21.3 fusion.288
  1540.2 10.8 exponential_reduce_fusion.2
  1560.4 21.3 fusion.288
  1581.7 10.8 exponential_reduce_fusion.2
  1601.9 21.3 fusion.288
  1623.3 10.8 exponential_reduce_fusion.2
  1643.5 12.7 pmax.7
  1676.2 48.1 %broadcast_in_dim.242 = f32[4,12800,768]{2,1,0:T(8,128)} broadcast(f32[]{:T(128)} %constant.273.clone.1), dimensions={} | broadcast | bytes 157286400 | tf_op jit(solution)/shard_map/broadcast_in_dim | solution.py:357
  1724.3 320.8 %while.39 = (s32[]{:T(128)}, f32[4,12800,768]{2,1,0:T(8,128)}, f32[4,128,768]{2,1,0:T(8,128)}, s32[4]{0:T(128)S(1)}, s32[512]{0:T(512)S(1)}, /*index=5*/f32[512]...) while((s32[]{:T(128)}, f32[4,12800,768]{2,1,0:T(8,128)}, ...), condition=%wide.region_28.29_spmd.clone, body=%wide.region_27.28_spmd.clone.sunk | while | flops 7571046400 | bytes 207235280 | solution.py:358
  1728.1 26.9 constant_dynamic-slice_fusion.30
  1756.6 10.5 fusion.296
  1767.2 28.5 bitcast_dynamic-update-slice_fusion.2
  1808.2 26.9 constant_dynamic-slice_fusion.30
  1836.8 10.5 fusion.296
  1847.3 28.6 bitcast_dynamic-update-slice_fusion.2
  1888.4 26.9 constant_dynamic-slice_fusion.30
  1917.0 10.5 fusion.296
  1927.5 28.6 bitcast_dynamic-update-slice_fusion.2
  1968.6 26.9 constant_dynamic-slice_fusion.30
  1997.2 10.5 fusion.296
  2007.7 28.6 bitcast_dynamic-update-slice_fusion.2
  2064.3 14.8 reduce-scatter.3.cloned.1.call-done
  2122.5 46.9 %broadcast_select_fusion = f32[4,9344,768]{2,0,1:T(4,128)} fusion(f32[9344,768]{1,0:T(8,128)} %get-tuple-element.393, pred[4]{0:T(512)(128)(4,1)S(1)} %copy-done.64), kind=kLoop, calls=%fused_computation.140 | loop fusion | flops 28704768 | bytes 143523840 | tf_op jit(solution)/shard_map/jit(_where)/select_n | solution.py:376
  2170.0 18.3 all_gather.27
  2188.4 75.4 %scatter_fusion = f32[4,12800,768]{2,1,0:T(8,128)} fusion(f32[4,12800,768]{2,1,0:T(8,128)} %get-tuple-element.154, s32[512]{0:T(512)S(1)} %bitcast.358, f32[512,768]{1,0:T(8,128)S(1)} %convert_element_type.245), kind=kCustom, calls=%fused_computation.2 | custom fusion | flops 393216 | bytes 4722688 | tf_op jit(solution)/shard_map/scatter-add | solution.py:370
  2263.9 78.0 %convert_element_type.246 = bf16[4,12800,768]{2,1,0:T(8,128)(2,1)} convert(f32[4,12800,768]{2,1,0:T(8,128)} %scatter_fusion) | non-fusion elementwise | flops 39321600 | bytes 235929600 | tf_op jit(solution)/shard_map/convert_element_type | solution.py:374
  2344.4 39.1 psum.38
  2386.6 1602.7 %all-reduce.11.cloned.1.call-done = f32[4,9344,768]{2,0,1:T(4,128)} async-done(((f32[4,9344,768]{2,0,1:T(4,128)}), f32[4,9344,768]{2,0,1:T(4,128)}) %all-reduce.11.cloned.1.call-update) | async-done | bytes 114819088
  3997.5 37.0 multiply_subtract_fusion
  (488 shorter events, 342.1 us)
Async XLA Ops:
  8.0 1045.8 %all-reduce.9.cloned.1.call-start = ((), (), s32[]{:S(2)}) async-start(), calls=%async_computation.7 | async-start | bytes 6291456
  8.1 30.5 copy-start.2
  38.6 669.5 %copy-start.69 = (s32[1,128]{1,0:T(1,128)S(1)}, s32[1,128]{1,0:T(1,128)}, u32[]{:S(2)}) copy-start(s32[1,128]{1,0:T(1,128)} %param.16) | copy-start | bytes 1540
  65.2 212.5 %collective-permute-start = (bf16[4,1600,768]{2,0,1:T(4,128)(2,1)S(1)}, bf16[4,1600,768]{2,0,1:T(4,128)(2,1)S(1)}, u32[]{:S(2)}, u32[]{:S(2)}) collective-permute-start(bf16[4,1600,768]{2,0,1:T(4,128)(2,1)S(1)} %get-tuple-element.386), channel_id=1, source_target_pairs={{0,4},{4,8},{8,12},{12,16},{16,20},{20,24},{24,28},{28,0},{1,5},{5... | collective-permute-start | bytes 29491208 | tf_op jit(solution)/shard_map/ppermute | solution.py:269
  65.6 216.7 %collective-permute-start.1 = (bf16[4,1600,768]{2,0,1:T(4,128)(2,1)S(1)}, bf16[4,1600,768]{2,0,1:T(4,128)(2,1)S(1)}, u32[]{:S(2)}, u32[]{:S(2)}) collective-permute-start(bf16[4,1600,768]{2,0,1:T(4,128)(2,1)S(1)} %get-tuple-element.386), channel_id=1, source_target_pairs={{0,28},{4,0},{8,4},{12,8},{16,12},{20,16},{24,20},{28,24},{1,29},{... | collective-permute-start | bytes 29491208 | tf_op jit(solution)/shard_map/ppermute | solution.py:272
  281.5 211.8 %collective-permute-start.2 = (bf16[4,1600,768]{2,0,1:T(4,128)(2,1)S(1)}, bf16[4,1600,768]{2,0,1:T(4,128)(2,1)S(1)}, u32[]{:S(2)}, u32[]{:S(2)}) collective-permute-start(bf16[4,1600,768]{2,0,1:T(4,128)(2,1)S(1)} %collective-permute-done), channel_id=1, source_target_pairs={{0,4},{4,8},{8,12},{12,16},{16,20},{20,24},{24,28},{28,0},{1,5},{5... | collective-permute-start | bytes 29491208 | tf_op jit(solution)/shard_map/ppermute | solution.py:269
  282.3 211.1 %copy-start.5 = (bf16[4,1600,768]{2,0,1:T(4,128)(2,1)}, bf16[4,1600,768]{2,0,1:T(4,128)(2,1)S(1)}, u32[]{:S(2)}) copy-start(bf16[4,1600,768]{2,0,1:T(4,128)(2,1)S(1)} %collective-permute-done.1) | copy-start | bytes 29491204
  282.3 213.6 %collective-permute-start.3 = (bf16[4,1600,768]{2,0,1:T(4,128)(2,1)S(1)}, bf16[4,1600,768]{2,0,1:T(4,128)(2,1)}, u32[]{:S(2)}, u32[]{:S(2)}) collective-permute-start(bf16[4,1600,768]{2,0,1:T(4,128)(2,1)S(1)} %collective-permute-done.1), channel_id=1, source_target_pairs={{0,28},{4,0},{8,4},{12,8},{16,12},{20,16},{24,20},{28,24},{1,29},{... | collective-permute-start | bytes 29491208 | tf_op jit(solution)/shard_map/ppermute | solution.py:272
  493.4 211.4 %collective-permute-start.4 = (bf16[4,1600,768]{2,0,1:T(4,128)(2,1)S(1)}, bf16[4,1600,768]{2,0,1:T(4,128)(2,1)}, u32[]{:S(2)}, u32[]{:S(2)}) collective-permute-start(bf16[4,1600,768]{2,0,1:T(4,128)(2,1)S(1)} %collective-permute-done.2), channel_id=1, source_target_pairs={{0,4},{4,8},{8,12},{12,16},{16,20},{20,24},{24,28},{28,0},{1,5},{5... | collective-permute-start | bytes 29491208 | tf_op jit(solution)/shard_map/ppermute | solution.py:269
  497.2 267.6 %collective-permute-start.5 = (bf16[4,1600,768]{2,0,1:T(4,128)(2,1)}, bf16[4,1600,768]{2,0,1:T(4,128)(2,1)}, u32[]{:S(2)}, u32[]{:S(2)}) collective-permute-start(bf16[4,1600,768]{2,0,1:T(4,128)(2,1)} %collective-permute-done.3), channel_id=1, source_target_pairs={{0,28},{4,0},{8,4},{12,8},{16,12},{20,16},{24,20},{28,24},{1,29},{... | collective-permute-start | bytes 29491208 | tf_op jit(solution)/shard_map/ppermute | solution.py:272
  704.8 109.5 %collective-permute-start.6 = (bf16[4,1600,768]{2,0,1:T(4,128)(2,1)}, bf16[4,1600,768]{2,0,1:T(4,128)(2,1)}, u32[]{:S(2)}, u32[]{:S(2)}) collective-permute-start(bf16[4,1600,768]{2,0,1:T(4,128)(2,1)} %collective-permute-done.4), channel_id=1, source_target_pairs={{0,4},{4,8},{8,12},{12,16},{16,20},{20,24},{24,28},{28,0},{1,5},{5... | collective-permute-start | bytes 29491208 | tf_op jit(solution)/shard_map/ppermute | solution.py:269
  708.1 27.7 slice-start
  722.8 13.1 slice-start.1
  722.8 18.4 slice-start.3
  722.8 18.4 slice-start.4
  845.6 403.3 %all-gather.7.cloned.1.call-start = ((), (), s32[]{:S(2)}) async-start(), calls=%async_computation.2 | async-start | bytes 59203584 | tf_op jit(solution)/shard_map/all_gather | solution.py:262
  849.5 627.8 %all-gather.9.cloned.1.call-start = ((), (), s32[]{:S(2)}) async-start(), calls=%async_computation.3 | async-start | bytes 3932160 | tf_op jit(solution)/shard_map/all_gather | solution.py:302
  1055.3 232.8 %copy-start.10 = (f32[4,14,768]{2,0,1:T(4,128)S(1)}, f32[4,14,768]{2,0,1:T(4,128)}, u32[]{:S(2)}) copy-start(f32[4,14,768]{2,0,1:T(4,128)} %param.24) | copy-start | bytes 516100
  1055.3 232.8 %copy-start.23 = (s32[1,128]{1,0:T(1,128)S(1)}, s32[1,128]{1,0:T(1,128)}, u32[]{:S(2)}) copy-start(s32[1,128]{1,0:T(1,128)} %param.18) | copy-start | bytes 1540
  1288.1 112.4 %copy-start.70 = (s32[1,128]{1,0:T(1,128)S(1)}, s32[1,128]{1,0:T(1,128)}, u32[]{:S(2)}) copy-start(s32[1,128]{1,0:T(1,128)} %param.17) | copy-start | bytes 1540
  1357.0 119.5 %copy-start = (f32[4,128,768]{2,1,0:T(8,128)}, f32[4,128,768]{2,1,0:T(8,128)S(1)}, u32[]{:S(2)}) copy-start(f32[4,128,768]{2,1,0:T(8,128)S(1)} %get-tuple-element.768) | copy-start | bytes 4718596
  1357.0 722.1 %reduce-scatter.3.cloned.1.call-start = ((), (), s32[]{:S(2)}) async-start(), calls=%async_computation.4 | async-start | bytes 1966080 | tf_op jit(solution)/shard_map/reduce_scatter | solution.py:359
  1400.5 22.2 copy-start.62
  1419.6 56.5 %copy-start.29 = (s32[4,1,128]{2,1,0:T(1,128)}, s32[4,1,128]{2,1,0:T(1,128)S(1)}, u32[]{:S(2)}) copy-start(s32[4,1,128]{2,1,0:T(1,128)S(1)} %all-gather.2) | copy-start | bytes 6148
  1420.3 56.2 %copy-start.21 = (f32[768]{0:T(1024)}, f32[768]{0:T(1024)S(1)}, u32[]{:S(2)}) copy-start(f32[768]{0:T(1024)S(1)} %get-tuple-element.306) | copy-start | bytes 9220
  1420.3 56.2 %copy-start.25 = (f32[768]{0:T(1024)}, f32[768]{0:T(1024)S(1)}, u32[]{:S(2)}) copy-start(f32[768]{0:T(1024)S(1)} %get-tuple-element.305) | copy-start | bytes 9220
  1477.3 188.0 %copy-start.74 = (f32[4]{0:T(128)S(1)}, f32[4]{0:T(128)}, u32[]{:S(2)}) copy-start(f32[4]{0:T(128)} %fusion.185) | copy-start | bytes 52
  1477.3 188.0 %copy-start.75 = (f32[128]{0:T(128)S(1)}, f32[128]{0:T(128)}, u32[]{:S(2)}) copy-start(f32[128]{0:T(128)} %pad_maximum_fusion.3) | copy-start | bytes 1540
  1477.3 188.6 %copy-start.72 = (f32[127]{0:T(128)S(1)}, f32[127]{0:T(128)}, u32[]{:S(2)}) copy-start(f32[127]{0:T(128)} %copy-done.71) | copy-start | bytes 1528
  1477.3 198.8 %copy-start.54 = (f32[512]{0:T(512)S(1)}, f32[512]{0:T(512)}, u32[]{:S(2)}) copy-start(f32[512]{0:T(512)} %select_reduce_fusion) | copy-start | bytes 6148
  1643.4 80.8 %copy-start.31 = (pred[512]{0:T(512)(128)(4,1)}, pred[512]{0:T(512)(128)(4,1)S(1)}, u32[]{:S(2)}) copy-start(pred[512]{0:T(512)(128)(4,1)S(1)} %get-tuple-element.797) | copy-start | bytes 1540
  1676.1 48.1 %copy-start.30 = (s32[4,1,128]{2,1,0:T(1,128)S(1)}, s32[4,1,128]{2,1,0:T(1,128)}, u32[]{:S(2)}) copy-start(s32[4,1,128]{2,1,0:T(1,128)} %copy-done.29) | copy-start | bytes 6148
  1724.3 321.3 %copy-start.9 = (bf16[128,768]{1,0:T(8,128)(2,1)S(1)}, bf16[128,768]{1,0:T(8,128)(2,1)}, u32[]{:S(2)}) copy-start(bf16[128,768]{1,0:T(8,128)(2,1)} %fusion.131) | copy-start | bytes 589828
  1724.3 321.3 %copy-start.37 = (f32[768]{0:T(1024)S(1)}, f32[768]{0:T(1024)}, u32[]{:S(2)}) copy-start(f32[768]{0:T(1024)} %get-tuple-element.304) | copy-start | bytes 9220
  1724.3 323.3 %copy-start.36 = (f32[768]{0:T(1024)S(1)}, f32[768]{0:T(1024)}, u32[]{:S(2)}) copy-start(f32[768]{0:T(1024)} %get-tuple-element.303) | copy-start | bytes 9220
  1728.1 28.5 copy-start.32
  1808.2 28.5 copy-start.32
  1888.4 28.5 copy-start.32
  1968.6 28.5 copy-start.32
  2045.1 339.6 %all-reduce.7.cloned.1.call-start = ((), (), s32[]{:S(2)}) async-start(), calls=%async_computation.6 | async-start | bytes 344064 | tf_op jit(solution)/shard_map/psum | solution.py:379
  2055.7 36.5 copy-start.49
  2060.0 19.1 copy-start.27
  2121.6 1867.6 %all-reduce.11.cloned.1.call-start = ((), (), s32[]{:S(2)}) async-start(), calls=%async_computation.8 | async-start | bytes 229638144
  2169.4 1828.1 %reduce-scatter.5.cloned.1.call-start = ((), (), s32[]{:S(2)}) async-start(), calls=%async_computation.5 | async-start | bytes 88473600 | tf_op jit(solution)/shard_map/reduce_scatter | solution.py:373
  2341.8 41.7 %copy-start.73 = (f32[4]{0:T(128)S(1)}, f32[4]{0:T(128)}, u32[]{:S(2)}) copy-start(f32[4]{0:T(128)} %get-tuple-element.308) | copy-start | bytes 52
  2341.8 42.8 %copy-start.11 = (f32[4,14,768]{2,0,1:T(4,128)S(1)}, f32[4,14,768]{2,0,1:T(4,128)}, u32[]{:S(2)}) copy-start(f32[4,14,768]{2,0,1:T(4,128)} %param.24) | copy-start | bytes 516100
  2341.9 42.8 %copy-start.20 = (f32[4,14,768]{2,0,1:T(4,128)S(1)}, f32[4,14,768]{2,0,1:T(4,128)}, u32[]{:S(2)}) copy-start(f32[4,14,768]{2,0,1:T(4,128)} %param.25) | copy-start | bytes 516100
  3997.5 37.0 copy-start.18
  (52 other events, 255.8 us)
Sparse Core Ops, SparseCore 0:
  845.7 208.1 all-reduce.8
  1357.1 62.5 all-gather.8
  2045.2 33.9 reduce-scatter.2
  2342.0 560.1 reduce-scatter.4
Sparse Core Ops, SparseCore 1:
  849.6 399.3 all-gather.6
  2121.7 121.0 all-reduce.6
  2250.2 1739.0 all-reduce.10
